TPU v7x, 256 devices: a whole 4x4x8 slice. The times are simulated.
256 devices in a mesh: group: 16 (over z, x_hi), expert: 16 (over x_lo, y, core).
Axes of the slice: x: 4 (x_hi: 2, x_lo: 2; x = x_hi * 2 + x_lo), y: 4, z: 8, core: 2. Of those that a mesh axis runs over, the one named last changes fastest.
Arguments:
- hidden_in: bfloat16 [16384, 2048], P(('group', 'expert')), may hold values from -54 to 54
- norm_attention: float32 [2048], replicated, may hold values from 0.5 to 1.5
- norm_experts: float32 [2048], replicated, may hold values from 0.5 to 1.5
- query_master: float32 [2048, 4096], P('group', 'expert'), may hold values from -0.125 to 0.125
- trainer_key_value_weight: float32 [2, 2048, 512], P(None, 'group'), may hold values from -0.125 to 0.125
- output_master: float32 [4096, 2048], P('expert', 'group'), may hold values from -0.09375 to 0.09375
- query_gain: float32 [128], replicated, may hold values from 0.5 to 1.5
- key_gain: float32 [128], replicated, may hold values from 0.5 to 1.5
- lengths: int32 [8], replicated, may hold values from 1 to 2048, as said below
- router: bfloat16 [2048, 128], replicated, may hold values from -0.125 to 0.125
- expert_gateup: bfloat16 [16, 2048, 1536], P('expert'), may hold values from -0.125 to 0.125
- expert_down: bfloat16 [16, 768, 2048], P('expert'), may hold values from -0.21875 to 0.21875
- routes: int32 [16384, 8], P(('group', 'expert')), may hold values from 0 to 127, as said below
Outputs:
- hidden: bfloat16 [16384, 2048], P(('group', 'expert'))
- expert_mix: bfloat16 [16384, 2048], P(('group', 'expert'))
Inputs may be any that keep to these rules, and one draw needn't show every extreme that they name: `lengths`: one request has exactly 2048 valid tokens. `routes`: A row's 8 experts are different, and at most one of them is below 16. In the 64 rows of one device, each expert below 16 is named by at most 4 rows; in every such block some expert is named by exactly 4 rows, and one expert is named by exactly 4 rows in every block.
All inputs are finite; a program needn't handle non-finite values.
Results may differ from a plain program's by a relative error of at most 0.02.
Values may be sent and summed in bfloat16 or wider, within the bound.
A program may use at most 64 MiB of HBM per device.

v0:
```python
import math
import jax
import jax.numpy as jnp
from jax import lax
from jax.sharding import PartitionSpec as P

QUERY_HEADS = 32
KEY_VALUE_HEADS = 4
HEAD_DIMENSION = 128
epsilon = 1e-06
rope_theta = 1000000.0


def from_partner(block, axis, stride):
    count = lax.axis_size(axis)
    route = []
    for low in range(count):
        high = low | 1 << stride
        if high != low and high < count:
            route += [(low, high), (high, low)]
    return lax.ppermute(block, axis, route)


def norm_rows(values, gain_vector):
    widened = values.astype(jnp.float32)
    inverse_rms = lax.rsqrt(jnp.mean(widened * widened, axis=-1, keepdims=True) + epsilon)
    return widened * inverse_rms * gain_vector


def rotate(values, positions):
    half_width = values.shape[-1] // 2
    exponents = jnp.arange(half_width).astype(jnp.float32)
    inverse = jnp.exp(exponents * (-2.0 * math.log(rope_theta) / values.shape[-1]))
    angles = positions[:, None, None] * inverse[None, None, :]
    cosine_values = jnp.cos(angles)
    sine_values = jnp.sin(angles)
    first_half = values[..., :half_width]
    second = values[..., half_width:]
    return jnp.concatenate(
        [
            first_half * cosine_values - second * sine_values,
            second * cosine_values + first_half * sine_values,
        ],
        axis=-1,
    )


def local_positions(parity, row_count):
    indices = jnp.arange(row_count)
    quarter = row_count // 2
    offset = jnp.where(parity == 0, jnp.where(indices < quarter, 0, 2 * quarter), quarter)
    return indices + offset


def per_device(
    hidden_in,
    norm_attention,
    norm_experts,
    query_master,
    trainer_key_value_weight,
    output_master,
    query_gain,
    key_gain,
    lengths,
    router,
    expert_gateup,
    expert_down,
    routes,
):
    experts_axis = lax.axis_size("expert")
    group_member = lax.axis_index("expert")
    group_index = lax.axis_index("group")
    local_head_count = QUERY_HEADS // experts_axis
    width_here = local_head_count * HEAD_DIMENSION
    common_head = group_member * local_head_count // (QUERY_HEADS // KEY_VALUE_HEADS)
    keyvalue_slice = lax.dynamic_slice_in_dim(
        trainer_key_value_weight, common_head * HEAD_DIMENSION, HEAD_DIMENSION, 2
    ).astype(jnp.bfloat16)
    query_full, keyvalue_full, output_part = (
        lax.all_gather(query_master.astype(jnp.bfloat16), "group", axis=0, tiled=True),
        lax.all_gather(keyvalue_slice, "group", axis=1, tiled=True),
        lax.all_gather(output_master.astype(jnp.bfloat16), "group", axis=1, tiled=True),
    )
    joined_weights = jnp.concatenate([query_full, keyvalue_full[0], keyvalue_full[1]], axis=1)
    normed = norm_rows(hidden_in, norm_attention).astype(jnp.bfloat16)
    projected = jnp.dot(
        lax.all_gather(normed, "expert", axis=0, tiled=True),
        joined_weights,
        preferred_element_type=jnp.float32,
    ).astype(jnp.bfloat16)
    local_rows = projected.shape[0]
    query_rows_list = projected[:, :width_here].reshape(
        local_rows, local_head_count, HEAD_DIMENSION
    )
    key_rows = projected[:, width_here : width_here + HEAD_DIMENSION]
    value_rows = projected[:, width_here + HEAD_DIMENSION :]
    parity = group_index % 2
    own_places = local_positions(parity, local_rows)
    partner_places = local_positions(1 - parity, local_rows)
    query_rows_list = rotate(
        norm_rows(query_rows_list, query_gain), own_places.astype(jnp.float32)
    ).astype(jnp.bfloat16)
    key_rows = rotate(norm_rows(key_rows[:, None, :], key_gain), own_places.astype(jnp.float32))[
        :, 0, :
    ].astype(jnp.bfloat16)
    partner = from_partner(jnp.stack([key_rows, value_rows]), "group", 0)
    all_keys = jnp.concatenate([key_rows, partner[0]], axis=0)
    all_values = jnp.concatenate([value_rows, partner[1]], axis=0)
    key_places = jnp.concatenate([own_places, partner_places])
    valid_length = jnp.sum(jnp.where(jnp.arange(lengths.shape[0]) == group_index // 2, lengths, 0))
    block_rows = min(512, local_rows)
    block_count = local_rows // block_rows
    score_scale = HEAD_DIMENSION ** (-0.5)

    def attend(block_index):
        block_start = block_index * block_rows
        query_block = lax.dynamic_slice_in_dim(query_rows_list, block_start, block_rows, 0)
        query_places = lax.dynamic_slice_in_dim(own_places, block_start, block_rows, 0)
        scores = (
            jnp.einsum("qhd,kd->hqk", query_block, all_keys, preferred_element_type=jnp.float32)
            * score_scale
        )
        allowed = (key_places[None, :] <= query_places[:, None]) & (
            key_places[None, :] < valid_length
        )
        weights = jnp.where(allowed[None], jnp.exp(scores), 0.0)
        denominators = jnp.sum(weights, axis=-1)
        weighted = jnp.einsum(
            "hqk,kd->qhd",
            weights.astype(jnp.bfloat16),
            all_values,
            preferred_element_type=jnp.float32,
        )
        return (weighted / jnp.transpose(denominators)[:, :, None]).astype(jnp.bfloat16)

    attended = lax.map(attend, jnp.arange(block_count)).reshape(local_rows, width_here)
    summed = lax.psum_scatter(
        jnp.dot(attended, output_part, preferred_element_type=jnp.float32).astype(jnp.bfloat16),
        "expert",
        scatter_dimension=0,
        tiled=True,
    ).astype(jnp.float32)
    hidden = (hidden_in.astype(jnp.float32) + summed).astype(jnp.bfloat16)
    normed_second = norm_rows(hidden, norm_experts).astype(jnp.bfloat16)
    logits = jnp.dot(normed_second, router, preferred_element_type=jnp.float32)
    route_table = routes[:, :, None] == jnp.arange(logits.shape[1])[None, None, :]
    picked = jnp.sum(jnp.where(route_table, logits[:, None, :], 0.0), axis=-1)
    raised = jnp.exp(picked)
    gate_values = raised / jnp.sum(raised, axis=1, keepdims=True)
    inside = routes < experts_axis
    gate_window = jnp.sum(jnp.where(inside, gate_values, 0.0), axis=1)
    expert_window = jnp.sum(jnp.where(inside, routes, 0), axis=1)
    present = jnp.any(inside, axis=1)
    capacity = local_rows // (experts_axis * experts_axis)
    member_table = (
        present[:, None] & (expert_window[:, None] == jnp.arange(experts_axis)[None, :])
    ).astype(jnp.int32)
    ranking = jnp.sum(jnp.cumsum(member_table, axis=0) * member_table, axis=1) - 1
    slot_index = expert_window * capacity + ranking
    select = (
        (jnp.arange(experts_axis * capacity)[:, None] == slot_index[None, :]) & present[None, :]
    ).astype(jnp.bfloat16)
    model_width = normed_second.shape[1]
    outgoing = (
        jnp.dot(select, normed_second, preferred_element_type=jnp.float32)
        .astype(jnp.bfloat16)
        .reshape(experts_axis, capacity, model_width)
    )
    gateup_here = expert_gateup[0]
    down_here = expert_down[0]
    hidden_units = down_here.shape[0]
    slot_items = lax.all_to_all(outgoing, "expert", split_axis=0, concat_axis=0, tiled=True)
    flattened = slot_items.reshape(-1, slot_items.shape[-1])
    gate_up = jnp.dot(flattened, gateup_here, preferred_element_type=jnp.float32)
    active = (jax.nn.silu(gate_up[:, :hidden_units]) * gate_up[:, hidden_units:]).astype(
        jnp.bfloat16
    )
    result = (
        jnp.dot(active, down_here, preferred_element_type=jnp.float32)
        .astype(jnp.bfloat16)
        .reshape(slot_items.shape)
    )
    returned = lax.all_to_all(result, "expert", split_axis=0, concat_axis=0, tiled=True)
    combined = jnp.dot(
        jnp.transpose(select), returned.reshape(-1, model_width), preferred_element_type=jnp.float32
    )
    expert_mix = (gate_window[:, None] * combined).astype(jnp.bfloat16)
    return (hidden, expert_mix)


def solution(mesh):
    return jax.shard_map(
        per_device,
        mesh=mesh,
        in_specs=(
            P(("group", "expert"), None),
            P(),
            P(),
            P("group", "expert"),
            P(None, "group", None),
            P("expert", "group"),
            P(),
            P(),
            P(),
            P(),
            P("expert", None, None),
            P("expert", None, None),
            P(("group", "expert"), None),
        ),
        out_specs=(P(("group", "expert"), None), P(("group", "expert"), None)),
        check_vma=False,
    )
```

profile of v0, /device:TPU:1, one launch (start us, length us, event | category | flops | bytes accessed | tf_op | source)
XLA Modules:
  0.0 400.9 jit_solution(13658261090532443639)
XLA Ops:
  7.2 1.7 dynamic-slice_convert_fusion
  9.0 1.5 convert_element_type.103
  10.6 1.1 fusion.36
  11.7 1.8 fusion.38
  13.6 1.5 convert_element_type.114
  15.3 3.1 multiply_cosine_fusion
  18.4 1.4 fusion.68
  19.7 69.8 %all-gather.9.cloned.1.call-done = bf16[2,2048,128]{2,1,0:T(8,128)(2,1)} async-done(((bf16[2,128,128]{2,1,0:T(8,128)(2,1)}), bf16[2,2048,128]{2,1,0:T(8,128)(2,1)}) %all-gather.9.cloned.1.call-update) | async-done | bytes 1048592 | tf_op jit(solution)/shard_map/all_gather | solution.py:81
  89.6 2.3 slice_bitcast_fusion.1
  91.9 75.7 %all-gather.7.cloned.1.call-done = bf16[2048,256]{1,0:T(8,128)(2,1)} async-done(((bf16[128,256]{1,0:T(8,128)(2,1)}), bf16[2048,256]{1,0:T(8,128)(2,1)}) %all-gather.7.cloned.1.call-update) | async-done | bytes 1048592 | tf_op jit(solution)/shard_map/all_gather | solution.py:80
  167.6 43.1 %all-gather.5.cloned.1.call-done = bf16[1024,2048]{1,0:T(8,128)(2,1)} async-done(((bf16[64,2048]{1,0:T(8,128)(2,1)}), bf16[1024,2048]{1,0:T(8,128)(2,1)}) %all-gather.5.cloned.1.call-update) | async-done | bytes 4194320 | tf_op jit(solution)/shard_map/all_gather | solution.py:87
  210.7 5.2 %fusion.27 = bf16[1024,512]{0,1:T(8,128)(2,1)S(1)} fusion(bf16[1024,2048]{1,0:T(8,128)(2,1)} %all-gather.5.cloned.1.call-done, bf16[2048,128]{1,0:T(8,128)(2,1)} %get-tuple-element.104, bf16[2048,128]{1,0:T(8,128)(2,1)} %get-tuple-element.103, bf16[2048,256]{1,0:T(8,128)(2,1)} %all-gather.7.cloned.1.call-done), kind=kOutput, calls=%fused_computation.34 | convolution fusion | flops 2154299392 | bytes 7340032 | tf_op jit(solution)/shard_map/dot_general | solution.py:86
  216.0 0.8 slice.54
  216.8 0.1 multiply_reduce_fusion
  217.1 1.2 fusion.46
  218.2 0.7 fusion.55
  219.0 0.9 pad_maximum_fusion.1
  219.8 2.4 collective-permute-start
  222.3 2.2 copy.24
  224.5 1.6 multiply_multiply_fusion
  226.1 1.7 subtract_convert_fusion
  227.8 1.1 pad_maximum_fusion
  228.9 6.7 %collective-permute-done = bf16[2,1024,128]{1,2,0:T(8,128)(2,1)} collective-permute-done((bf16[2,1024,128]{1,2,0:T(8,128)(2,1)}, bf16[2,1024,128]{1,2,0:T(8,128)(2,1)}, u32[]{:S(2)}, u32[]{:S(2)}) %collective-permute-start) | collective-permute-done | bytes 524320 | tf_op jit(solution)/shard_map/ppermute | solution.py:21
  235.6 1.1 slice_bitcast_fusion.2
  236.7 1.1 pad_maximum_fusion.2
  237.8 2.1 copy.25
  239.8 2.1 copy.26
  241.9 19.4 %while.10 = (s32[]{:T(128)}, bf16[2,512,2,128]{3,2,1,0:T(2,128)(2,1)}, s32[2048]{0:T(1024)S(1)}, s32[2]{0:T(128)S(1)}, s32[1024]{0:T(1024)S(1)}, /*index=5*/s32[...) while((s32[]{:T(128)}, ...), condition=%wide.region_6.7_spmd, body=%wide.region_4.6_spmd.sunk | while | flops 1088685056 | bytes 24152800 | solution.py:136
  241.9 0.6 dynamic_slice.23
  243.2 0.7 broadcast_compare_fusion.3
  243.9 0.7 compare_and_fusion.2
  244.6 3.9 bitcast_reduce_fusion.2
  248.5 2.0 fusion.82
  250.6 1.0 copy_dynamic-update-slice_fusion.2
  251.6 0.6 dynamic_slice.23
  252.9 0.7 broadcast_compare_fusion.3
  253.6 0.7 compare_and_fusion.2
  254.3 3.9 bitcast_reduce_fusion.2
  258.2 2.0 fusion.82
  260.3 1.0 copy_dynamic-update-slice_fusion.2
  261.3 24.7 %all-gather.11.cloned.1.call-done = bf16[256,2048]{1,0:T(8,128)(2,1)} async-done(((bf16[256,128]{1,0:T(8,128)(2,1)}), bf16[256,2048]{1,0:T(8,128)(2,1)}) %all-gather.11.cloned.1.call-update) | async-done | bytes 1048592 | tf_op jit(solution)/shard_map/all_gather | solution.py:82
  286.0 4.6 %convolution_convert_fusion = bf16[1024,2048]{1,0:T(8,128)(2,1)} fusion(bf16[256,2048]{1,0:T(8,128)(2,1)} %all-gather.11.cloned.1.call-done, bf16[128,8,2,128]{3,2,1,0:T(2,128)(2,1)} %bitcast.20), kind=kOutput, calls=%fused_computation.21 | convolution fusion | flops 1075838976 | bytes 5767168 | tf_op jit(solution)/shard_map/dot_general | solution.py:138
  290.7 0.1 fusion.71
  290.8 0.1 select_reduce_fusion.2
  291.1 0.2 select_reduce_fusion.1
  291.3 64.7 %reduce-scatter.2.cloned.1.call-done = bf16[64,2048]{1,0:T(8,128)(2,1)} async-done(((bf16[1024,2048]{1,0:T(8,128)(2,1)}), bf16[64,2048]{1,0:T(8,128)(2,1)}) %reduce-scatter.2.cloned.1.call-update) | async-done | bytes 262160 | tf_op jit(solution)/shard_map/reduce_scatter | solution.py:137
  356.0 1.1 fusion.33
  357.2 0.7 copy-done.2
  357.9 0.3 convolution_convert_fusion.1
  358.2 0.8 reshape.264
  359.0 7.5 %all-to-all-start = ((bf16[16,4,2048]{2,1,0:T(4,128)(2,1)}), bf16[16,4,2048]{2,1,0:T(4,128)(2,1)S(1)}, u32[]{:S(2)}, u32[]{:S(2)}) async-start(bf16[16,4,2048]{2,1,0:T(4,128)(2,1)} %reshape.264), calls=%async_computation.1 | async-start | bytes 524288 | tf_op jit(solution)/shard_map/all_to_all | solution.py:172
  366.5 1.4 fusion.52
  367.9 5.8 %all-to-all-done = bf16[16,4,2048]{2,1,0:T(4,128)(2,1)S(1)} async-done(((bf16[16,4,2048]{2,1,0:T(4,128)(2,1)}), bf16[16,4,2048]{2,1,0:T(4,128)(2,1)S(1)}, u32[]{:S(2)}, u32[]{:S(2)}) %all-to-all-start) | async-done | bytes 262176 | tf_op jit(solution)/shard_map/all_to_all | solution.py:172
  373.8 0.8 reshape.265
  374.5 4.0 %fusion.13 = f32[64,1536]{1,0:T(8,128)S(1)} fusion(bf16[64,2048]{1,0:T(8,128)(2,1)} %reshape.265, bf16[1,2048,1536]{2,1,0:T(8,128)(2,1)} %param.25), kind=kOutput, calls=%fused_computation.19 | convolution fusion | flops 402653184 | bytes 6946816 | tf_op jit(solution)/shard_map/dot_general | solution.py:174
  378.6 0.7 fusion.18
  379.3 0.8 reshape.266
  380.1 4.9 %all-to-all-start.1 = ((bf16[16,4,2048]{2,1,0:T(4,128)(2,1)}), bf16[16,4,2048]{2,1,0:T(4,128)(2,1)}, u32[]{:S(2)}, u32[]{:S(2)}) async-start(bf16[16,4,2048]{2,1,0:T(4,128)(2,1)} %reshape.266), calls=%async_computation.2 | async-start | bytes 524288 | tf_op jit(solution)/shard_map/all_to_all | solution.py:183
  385.0 0.2 select_reduce_fusion
  385.2 0.1 exponential_reduce_fusion
  385.3 0.2 select_reduce_fusion.3
  385.5 6.8 %all-to-all-done.1 = bf16[16,4,2048]{2,1,0:T(4,128)(2,1)} async-done(((bf16[16,4,2048]{2,1,0:T(4,128)(2,1)}), bf16[16,4,2048]{2,1,0:T(4,128)(2,1)}, u32[]{:S(2)}, u32[]{:S(2)}) %all-to-all-start.1) | async-done | bytes 262176 | tf_op jit(solution)/shard_map/all_to_all | solution.py:183
  392.3 1.0 reshape.267
  393.4 1.0 fusion.17
  (48 shorter events, 1.0 us)
Async XLA Ops:
  7.2 371.4 %copy-start = (bf16[1,768,2048]{2,1,0:T(8,128)(2,1)S(1)}, bf16[1,768,2048]{2,1,0:T(8,128)(2,1)}, u32[]{:S(2)}) copy-start(bf16[1,768,2048]{2,1,0:T(8,128)(2,1)} %param.26) | copy-start | bytes 9437188
  7.2 82.4 %all-gather.9.cloned.1.call-start = ((), (), s32[]{:S(2)}) async-start(), calls=%async_computation.5 | async-start | bytes 1114112 | tf_op jit(solution)/shard_map/all_gather | solution.py:81
  9.0 158.6 %all-gather.7.cloned.1.call-start = ((), (), s32[]{:S(2)}) async-start(), calls=%async_computation.4 | async-start | bytes 1114112 | tf_op jit(solution)/shard_map/all_gather | solution.py:80
  10.6 200.1 %all-gather.5.cloned.1.call-start = ((), (), s32[]{:S(2)}) async-start(), calls=%async_computation.3 | async-start | bytes 4456448 | tf_op jit(solution)/shard_map/all_gather | solution.py:87
  13.5 272.4 %all-gather.11.cloned.1.call-start = ((), (), s32[]{:S(2)}) async-start(), calls=%async_computation.6 | async-start | bytes 1114112 | tf_op jit(solution)/shard_map/all_gather | solution.py:82
  15.2 340.9 %reduce-scatter.2.cloned.1.call-start = ((), (), s32[]{:S(2)}) async-start(), calls=%async_computation.7 | async-start | bytes 4456448 | tf_op jit(solution)/shard_map/reduce_scatter | solution.py:137
  210.6 6.3 %copy-start.8 = (f32[128]{0:T(128)S(1)}, f32[128]{0:T(128)}, u32[]{:S(2)}) copy-start(f32[128]{0:T(128)} %param.22) | copy-start | bytes 1540
  215.8 8.7 %copy-start.7 = (f32[128]{0:T(128)S(1)}, f32[128]{0:T(128)}, u32[]{:S(2)}) copy-start(f32[128]{0:T(128)} %param.21) | copy-start | bytes 1540
  219.8 15.8 %collective-permute-start = (bf16[2,1024,128]{1,2,0:T(8,128)(2,1)}, bf16[2,1024,128]{1,2,0:T(8,128)(2,1)}, u32[]{:S(2)}, u32[]{:S(2)}) collective-permute-start(bf16[2,1024,128]{1,2,0:T(8,128)(2,1)} %pad_maximum_fusion.1), channel_id=1, source_target_pairs={{0,16},{16,0},{32,48},{48,32},{64,80},{80,64},{96,112},{112,96},{1... | collective-permute-start | bytes 1572872 | tf_op jit(solution)/shard_map/ppermute | solution.py:21
  224.5 12.2 %copy-start.3 = (bf16[1024,128]{0,1:T(8,128)(2,1)S(1)}, bf16[1024,128]{0,1:T(8,128)(2,1)}, u32[]{:S(2)}) copy-start(bf16[1024,128]{0,1:T(8,128)(2,1)} %get-tuple-element.109) | copy-start | bytes 786436
  244.6 3.9 copy-start.4
  254.3 3.9 copy-start.4
  286.0 4.6 %copy-start.6 = (s32[64,8]{0,1:T(8,128)S(1)}, s32[64,8]{0,1:T(8,128)}, u32[]{:S(2)}) copy-start(s32[64,8]{0,1:T(8,128)} %param.27) | copy-start | bytes 6148
  290.6 65.5 %copy-start.1 = (bf16[64,2048]{1,0:T(8,128)(2,1)S(1)}, bf16[64,2048]{1,0:T(8,128)(2,1)}, u32[]{:S(2)}) copy-start(bf16[64,2048]{1,0:T(8,128)(2,1)} %param.15) | copy-start | bytes 786436
  290.6 67.3 %copy-start.5 = (f32[2048]{0:T(1024)S(1)}, f32[2048]{0:T(1024)}, u32[]{:S(2)}) copy-start(f32[2048]{0:T(1024)} %param.17) | copy-start | bytes 24580
  357.2 0.7 copy-start.2
  359.0 14.8 %all-to-all-start = ((bf16[16,4,2048]{2,1,0:T(4,128)(2,1)}), bf16[16,4,2048]{2,1,0:T(4,128)(2,1)S(1)}, u32[]{:S(2)}, u32[]{:S(2)}) async-start(bf16[16,4,2048]{2,1,0:T(4,128)(2,1)} %reshape.264), calls=%async_computation.1 | async-start | bytes 524288 | tf_op jit(solution)/shard_map/all_to_all | solution.py:172
  380.1 12.3 %all-to-all-start.1 = ((bf16[16,4,2048]{2,1,0:T(4,128)(2,1)}), bf16[16,4,2048]{2,1,0:T(4,128)(2,1)}, u32[]{:S(2)}, u32[]{:S(2)}) async-start(bf16[16,4,2048]{2,1,0:T(4,128)(2,1)} %reshape.266), calls=%async_computation.2 | async-start | bytes 524288 | tf_op jit(solution)/shard_map/all_to_all | solution.py:183
Sparse Core Ops, SparseCore 0:
  10.6 78.9 all-gather.8
  92.1 75.3 all-gather.6
  170.0 40.6 all-gather.4
  213.5 72.3 all-gather.10
  290.7 65.2 reduce-scatter.1
where the time goes:
time: 402 us; the launch traced here: 401 us
  waiting for transfers between devices  297 us (74%)
  matrix products  29 us (7%)
  other arithmetic  24.1 us (6%)
  local copies, waits for them, and re-layouts  19.8 us (5%)
  starting transfers between devices  15.1 us (4%)
  between operations  14.1 us (4%)
    all_gather x1, waiting for transfers between devices, per_device(): lax.all_gather(query_master.astype(jnp.bfloat16), 'group', axis=0, tiled=...  75.7 us
    all_gather x1, waiting for transfers between devices, per_device(): lax.all_gather(keyvalue_slice, 'group', axis=1, tiled=True)  69.8 us
    reduce_scatter x1, waiting for transfers between devices, per_device(): lax.psum_scatter(jnp.dot(attended, output_part, preferred_element_type=jn...  64.7 us
    all_gather x1, waiting for transfers between devices, per_device(): lax.all_gather(normed, 'expert', axis=0, tiled=True)  43.1 us
    all_gather x1, waiting for transfers between devices, per_device(): lax.all_gather(output_master.astype(jnp.bfloat16), 'group', axis=1, tiled...  24.7 us
  transfers between devices with their start and end apart: 8, of which 8 were waited for; matrix products, arithmetic and copies ran while one was open for 14% of the time, Pallas kernels for 0%

commit v1 on v0

--- a/solution.py
+++ b/solution.py
@@ -77,7 +77,15 @@
         trainer_key_value_weight, common_head * HEAD_DIMENSION, HEAD_DIMENSION, 2
     ).astype(jnp.bfloat16)
     query_full, keyvalue_full, output_part = (
-        lax.all_gather(query_master.astype(jnp.bfloat16), "group", axis=0, tiled=True),
+        jnp.concatenate(
+            lax.all_to_all(
+                jnp.stack(lax.axis_size("group") * [query_master.astype(jnp.bfloat16)]),
+                concat_axis=0,
+                axis_name="group",
+                split_axis=0,
+            ),
+            0,
+        ),
         lax.all_gather(keyvalue_slice, "group", axis=1, tiled=True),
         lax.all_gather(output_master.astype(jnp.bfloat16), "group", axis=1, tiled=True),
     )

time: 402 us -> 330 us (0.82)
  waiting for transfers between devices: 297 us -> 215 us
  starting transfers between devices: 15.1 us -> 26.6 us
    all_gather x1 -> x0, waiting for transfers between devices: 75.7 us -> none  [per_device(): lax.all_gather(query_master.astype(jnp.bfloat16), 'group', axis=0, tiled=...]
    all_to_all x0 -> x1, starting transfers between devices: none -> 11.6 us  [per_device(): lax.all_to_all(jnp.stack(lax.axis_size('group') * [query_master.astype(jn...]
    all_gather x1, waiting for transfers between devices: 69.8 us -> 65.1 us  [per_device(): lax.all_gather(keyvalue_slice, 'group', axis=1, tiled=True)]
  transfers between devices with their start and end apart: 8 -> 8, of which waited for: 8 -> 7; matrix products, arithmetic and copies ran while one was open for 14% -> 16% of each run, Pallas kernels for 0% -> 0%
where the time goes in v1:
time: 330 us; the launch traced here: 329 us
  waiting for transfers between devices  215 us (65%)
  matrix products  29 us (9%)
  starting transfers between devices  26.6 us (8%)
  other arithmetic  21.7 us (7%)
  local copies, waits for them, and re-layouts  20.9 us (6%)
  between operations  14.1 us (4%)
    all_gather x1, waiting for transfers between devices, per_device(): lax.all_gather(keyvalue_slice, 'group', axis=1, tiled=True)  65.1 us
    reduce_scatter x1, waiting for transfers between devices, per_device(): lax.psum_scatter(jnp.dot(attended, output_part, preferred_element_type=jn...  64.9 us
    all_gather x1, waiting for transfers between devices, per_device(): lax.all_gather(normed, 'expert', axis=0, tiled=True)  40.8 us
    all_gather x1, waiting for transfers between devices, per_device(): lax.all_gather(output_master.astype(jnp.bfloat16), 'group', axis=1, tiled...  25 us
    all_to_all x1, starting transfers between devices, per_device(): lax.all_to_all(jnp.stack(lax.axis_size('group') * [query_master.astype(jn...  11.6 us
    dot_general x2, matrix products, attend(): jnp.einsum('qhd,kd->hqk', query_block, all_keys, preferred_element_type=j...  7.79 us
    all_to_all x1, starting transfers between devices, per_device(): lax.all_to_all(outgoing, 'expert', split_axis=0, concat_axis=0, tiled=True)  7.51 us
    all_to_all x1, waiting for transfers between devices, per_device(): lax.all_to_all(result, 'expert', split_axis=0, concat_axis=0, tiled=True)  6.81 us
  transfers between devices with their start and end apart: 8, of which 7 were waited for; matrix products, arithmetic and copies ran while one was open for 16% of the time, Pallas kernels for 0%

profile of v1, /device:TPU:1, one launch (start us, length us, event | category | flops | bytes accessed | tf_op | source)
XLA Modules:
  0.0 328.9 jit_solution(655260516945171667)
XLA Ops:
  7.3 1.7 dynamic-slice_convert_fusion
  9.0 1.1 fusion.36
  10.1 1.8 fusion.38
  12.0 0.9 convert_element_type.103
  12.9 1.1 stack.6
  14.0 11.6 %all-to-all-start = ((bf16[16,128,256]{2,1,0:T(8,128)(2,1)}), bf16[16,128,256]{2,1,0:T(8,128)(2,1)}, u32[]{:S(2)}, u32[]{:S(2)}) async-start(bf16[16,128,256]{2,1,0:T(8,128)(2,1)} %stack.6), calls=%async_computation | async-start | bytes 2097152 | tf_op jit(solution)/shard_map/all_to_all | solution.py:81
  25.7 0.6 convert_element_type.114
  26.5 0.6 fusion.68
  27.1 3.1 multiply_cosine_fusion
  30.2 65.1 %all-gather.6.cloned.1.call-done = bf16[2,2048,128]{2,1,0:T(8,128)(2,1)} async-done(((bf16[2,128,128]{2,1,0:T(8,128)(2,1)}), bf16[2,2048,128]{2,1,0:T(8,128)(2,1)}) %all-gather.6.cloned.1.call-update) | async-done | bytes 1048592 | tf_op jit(solution)/shard_map/all_gather | solution.py:89
  95.3 2.3 slice_bitcast_fusion.1
  97.6 40.8 %all-gather.4.cloned.1.call-done = bf16[1024,2048]{1,0:T(8,128)(2,1)} async-done(((bf16[64,2048]{1,0:T(8,128)(2,1)}), bf16[1024,2048]{1,0:T(8,128)(2,1)}) %all-gather.4.cloned.1.call-update) | async-done | bytes 4194320 | tf_op jit(solution)/shard_map/all_gather | solution.py:95
  138.4 5.2 %fusion.27 = bf16[1024,512]{0,1:T(8,128)(2,1)S(1)} fusion(bf16[1024,2048]{1,0:T(8,128)(2,1)} %all-gather.4.cloned.1.call-done, bf16[2048,128]{1,0:T(8,128)(2,1)} %get-tuple-element.104, bf16[2048,128]{1,0:T(8,128)(2,1)} %get-tuple-element.103, bf16[2048,256]{1,0:T(8,128)(2,1)} %bitcast.7), kind=kOutput, calls=%fused_computation.34 | convolution fusion | flops 2154299392 | bytes 7340032 | tf_op jit(solution)/shard_map/dot_general | solution.py:94
  143.7 0.8 slice.54
  144.5 0.1 multiply_reduce_fusion
  144.8 1.2 fusion.46
  145.9 0.7 fusion.55
  146.7 0.9 pad_maximum_fusion.1
  147.5 2.4 collective-permute-start
  150.0 2.2 copy.24
  152.2 1.6 multiply_multiply_fusion
  153.8 1.7 subtract_convert_fusion
  155.5 1.1 pad_maximum_fusion
  156.6 6.7 %collective-permute-done = bf16[2,1024,128]{1,2,0:T(8,128)(2,1)} collective-permute-done((bf16[2,1024,128]{1,2,0:T(8,128)(2,1)}, bf16[2,1024,128]{1,2,0:T(8,128)(2,1)}, u32[]{:S(2)}, u32[]{:S(2)}) %collective-permute-start) | collective-permute-done | bytes 524320 | tf_op jit(solution)/shard_map/ppermute | solution.py:21
  163.3 1.1 slice_bitcast_fusion.2
  164.4 1.1 pad_maximum_fusion.2
  165.5 2.1 copy.25
  167.5 2.0 copy.26
  169.6 19.3 %while.10 = (s32[]{:T(128)}, bf16[2,512,2,128]{3,2,1,0:T(2,128)(2,1)}, s32[2048]{0:T(1024)S(1)}, s32[2]{0:T(128)S(1)}, s32[1024]{0:T(1024)S(1)}, /*index=5*/s32[...) while((s32[]{:T(128)}, ...), condition=%wide.region_6.7_spmd, body=%wide.region_4.6_spmd.sunk | while | flops 1088685056 | bytes 24152800 | solution.py:144
  169.6 0.6 dynamic_slice.23
  170.9 0.6 broadcast_compare_fusion.3
  171.5 0.7 compare_and_fusion.2
  172.3 3.9 %bitcast_reduce_fusion.2 = (f32[2,512]{1,0:T(2,128)S(1)}, f32[512,2,2048]{2,0,1:T(8,128)S(1)}) fusion(pred[512,2048]{1,0:T(8,128)(4,1)S(1)} %compare_and_fusion.2, bf16[2048,128]{1,0:T(8,128)(2,1)} %get-tuple-element.209, bf16[1024,2,128]{2,0,1:T(8,128)(2,1)} %get-tuple-element.208, s32[]{:T(128)S(6)} %select_n.131), kind=kOutput, calls=%fused_computation.clone.1 | convolution fusion | flops 543161344 | bytes 10227716 | tf_op jit(solution)/shard_map/while/body/eval_jaxpr/qhd,kd->hqk/dot_general | solution.py:128
  176.2 2.0 fusion.82
  178.2 1.0 copy_dynamic-update-slice_fusion.2
  179.2 0.6 dynamic_slice.23
  180.6 0.6 broadcast_compare_fusion.3
  181.2 0.7 compare_and_fusion.2
  182.0 3.9 %bitcast_reduce_fusion.2 = (f32[2,512]{1,0:T(2,128)S(1)}, f32[512,2,2048]{2,0,1:T(8,128)S(1)}) fusion(pred[512,2048]{1,0:T(8,128)(4,1)S(1)} %compare_and_fusion.2, bf16[2048,128]{1,0:T(8,128)(2,1)} %get-tuple-element.209, bf16[1024,2,128]{2,0,1:T(8,128)(2,1)} %get-tuple-element.208, s32[]{:T(128)S(6)} %select_n.131), kind=kOutput, calls=%fused_computation.clone.1 | convolution fusion | flops 543161344 | bytes 10227716 | tf_op jit(solution)/shard_map/while/body/eval_jaxpr/qhd,kd->hqk/dot_general | solution.py:128
  185.9 2.0 fusion.82
  187.9 1.0 copy_dynamic-update-slice_fusion.2
  188.9 25.0 %all-gather.8.cloned.1.call-done = bf16[256,2048]{1,0:T(8,128)(2,1)} async-done(((bf16[256,128]{1,0:T(8,128)(2,1)}), bf16[256,2048]{1,0:T(8,128)(2,1)}) %all-gather.8.cloned.1.call-update) | async-done | bytes 1048592 | tf_op jit(solution)/shard_map/all_gather | solution.py:90
  213.9 4.6 %convolution_convert_fusion = bf16[1024,2048]{1,0:T(8,128)(2,1)} fusion(bf16[256,2048]{1,0:T(8,128)(2,1)} %all-gather.8.cloned.1.call-done, bf16[128,8,2,128]{3,2,1,0:T(2,128)(2,1)} %bitcast.21), kind=kOutput, calls=%fused_computation.21 | convolution fusion | flops 1075838976 | bytes 5767168 | tf_op jit(solution)/shard_map/dot_general | solution.py:146
  218.7 0.1 select_reduce_fusion.2
  219.0 0.2 select_reduce_fusion.1
  219.2 64.9 %reduce-scatter.2.cloned.1.call-done = bf16[64,2048]{1,0:T(8,128)(2,1)} async-done(((bf16[1024,2048]{1,0:T(8,128)(2,1)}), bf16[64,2048]{1,0:T(8,128)(2,1)}) %reduce-scatter.2.cloned.1.call-update) | async-done | bytes 262160 | tf_op jit(solution)/shard_map/reduce_scatter | solution.py:145
  284.1 1.1 fusion.33
  285.3 0.7 copy-done.2
  286.0 0.3 convolution_convert_fusion.1
  286.3 0.8 reshape.270
  287.1 7.5 %all-to-all-start.1 = ((bf16[16,4,2048]{2,1,0:T(4,128)(2,1)}), bf16[16,4,2048]{2,1,0:T(4,128)(2,1)S(1)}, u32[]{:S(2)}, u32[]{:S(2)}) async-start(bf16[16,4,2048]{2,1,0:T(4,128)(2,1)} %reshape.270), calls=%async_computation.2 | async-start | bytes 524288 | tf_op jit(solution)/shard_map/all_to_all | solution.py:180
  294.6 1.4 fusion.52
  296.0 5.8 %all-to-all-done.1 = bf16[16,4,2048]{2,1,0:T(4,128)(2,1)S(1)} async-done(((bf16[16,4,2048]{2,1,0:T(4,128)(2,1)}), bf16[16,4,2048]{2,1,0:T(4,128)(2,1)S(1)}, u32[]{:S(2)}, u32[]{:S(2)}) %all-to-all-start.1) | async-done | bytes 262176 | tf_op jit(solution)/shard_map/all_to_all | solution.py:180
  301.8 0.8 reshape.271
  302.6 4.0 %fusion.13 = f32[64,1536]{1,0:T(8,128)S(1)} fusion(bf16[64,2048]{1,0:T(8,128)(2,1)} %reshape.271, bf16[1,2048,1536]{2,1,0:T(8,128)(2,1)} %param.25), kind=kOutput, calls=%fused_computation.19 | convolution fusion | flops 402653184 | bytes 6946816 | tf_op jit(solution)/shard_map/dot_general | solution.py:182
  306.7 0.7 fusion.18
  307.3 0.8 reshape.272
  308.1 4.9 %all-to-all-start.2 = ((bf16[16,4,2048]{2,1,0:T(4,128)(2,1)}), bf16[16,4,2048]{2,1,0:T(4,128)(2,1)}, u32[]{:S(2)}, u32[]{:S(2)}) async-start(bf16[16,4,2048]{2,1,0:T(4,128)(2,1)} %reshape.272), calls=%async_computation.3 | async-start | bytes 524288 | tf_op jit(solution)/shard_map/all_to_all | solution.py:191
  313.1 0.2 select_reduce_fusion
  313.3 0.1 exponential_reduce_fusion
  313.4 0.2 select_reduce_fusion.3
  313.6 6.8 %all-to-all-done.2 = bf16[16,4,2048]{2,1,0:T(4,128)(2,1)} async-done(((bf16[16,4,2048]{2,1,0:T(4,128)(2,1)}), bf16[16,4,2048]{2,1,0:T(4,128)(2,1)}, u32[]{:S(2)}, u32[]{:S(2)}) %all-to-all-start.2) | async-done | bytes 262176 | tf_op jit(solution)/shard_map/all_to_all | solution.py:191
  320.4 1.0 reshape.273
  321.4 1.0 fusion.17
  (52 shorter events, 1.1 us)
Async XLA Ops:
  7.2 299.5 %copy-start = (bf16[1,768,2048]{2,1,0:T(8,128)(2,1)S(1)}, bf16[1,768,2048]{2,1,0:T(8,128)(2,1)}, u32[]{:S(2)}) copy-start(bf16[1,768,2048]{2,1,0:T(8,128)(2,1)} %param.26) | copy-start | bytes 9437188
  7.2 18.5 %copy-start.5 = (f32[256,128]{1,0:T(8,128)S(1)}, f32[256,128]{1,0:T(8,128)}, u32[]{:S(2)}) copy-start(f32[256,128]{1,0:T(8,128)} %param.20) | copy-start | bytes 393220
  7.2 19.3 %copy-start.10 = (s32[8]{0:T(128)S(1)}, s32[8]{0:T(128)}, u32[]{:S(2)}) copy-start(s32[8]{0:T(128)} %param.23) | copy-start | bytes 100
  7.2 88.1 %all-gather.6.cloned.1.call-start = ((), (), s32[]{:S(2)}) async-start(), calls=%async_computation.5 | async-start | bytes 1114112 | tf_op jit(solution)/shard_map/all_gather | solution.py:89
  9.0 129.4 %all-gather.4.cloned.1.call-start = ((), (), s32[]{:S(2)}) async-start(), calls=%async_computation.4 | async-start | bytes 4456448 | tf_op jit(solution)/shard_map/all_gather | solution.py:95
  14.0 83.6 %all-to-all-start = ((bf16[16,128,256]{2,1,0:T(8,128)(2,1)}), bf16[16,128,256]{2,1,0:T(8,128)(2,1)}, u32[]{:S(2)}, u32[]{:S(2)}) async-start(bf16[16,128,256]{2,1,0:T(8,128)(2,1)} %stack.6), calls=%async_computation | async-start | bytes 2097152 | tf_op jit(solution)/shard_map/all_to_all | solution.py:81
  25.6 188.3 %all-gather.8.cloned.1.call-start = ((), (), s32[]{:S(2)}) async-start(), calls=%async_computation.6 | async-start | bytes 1114112 | tf_op jit(solution)/shard_map/all_gather | solution.py:90
  26.3 257.8 %reduce-scatter.2.cloned.1.call-start = ((), (), s32[]{:S(2)}) async-start(), calls=%async_computation.7 | async-start | bytes 4456448 | tf_op jit(solution)/shard_map/reduce_scatter | solution.py:145
  138.4 6.3 %copy-start.9 = (f32[128]{0:T(128)S(1)}, f32[128]{0:T(128)}, u32[]{:S(2)}) copy-start(f32[128]{0:T(128)} %param.22) | copy-start | bytes 1540
  143.6 8.6 %copy-start.8 = (f32[128]{0:T(128)S(1)}, f32[128]{0:T(128)}, u32[]{:S(2)}) copy-start(f32[128]{0:T(128)} %param.21) | copy-start | bytes 1540
  147.5 15.8 %collective-permute-start = (bf16[2,1024,128]{1,2,0:T(8,128)(2,1)}, bf16[2,1024,128]{1,2,0:T(8,128)(2,1)}, u32[]{:S(2)}, u32[]{:S(2)}) collective-permute-start(bf16[2,1024,128]{1,2,0:T(8,128)(2,1)} %pad_maximum_fusion.1), channel_id=1, source_target_pairs={{0,16},{16,0},{32,48},{48,32},{64,80},{80,64},{96,112},{112,96},{1... | collective-permute-start | bytes 1572872 | tf_op jit(solution)/shard_map/ppermute | solution.py:21
  152.2 12.2 %copy-start.3 = (bf16[1024,128]{0,1:T(8,128)(2,1)S(1)}, bf16[1024,128]{0,1:T(8,128)(2,1)}, u32[]{:S(2)}) copy-start(bf16[1024,128]{0,1:T(8,128)(2,1)} %get-tuple-element.109) | copy-start | bytes 786436
  172.3 3.9 %copy-start.4 = (bf16[2048,128]{1,0:T(8,128)(2,1)S(1)}, bf16[2048,128]{1,0:T(8,128)(2,1)}, u32[]{:S(2)}) copy-start(bf16[2048,128]{1,0:T(8,128)(2,1)} %get-tuple-element.210) | copy-start | bytes 1572868 | tf_op jit(solution)/shard_map/while
  181.9 3.9 %copy-start.4 = (bf16[2048,128]{1,0:T(8,128)(2,1)S(1)}, bf16[2048,128]{1,0:T(8,128)(2,1)}, u32[]{:S(2)}) copy-start(bf16[2048,128]{1,0:T(8,128)(2,1)} %get-tuple-element.210) | copy-start | bytes 1572868 | tf_op jit(solution)/shard_map/while
  213.9 4.6 %copy-start.7 = (s32[64,8]{0,1:T(8,128)S(1)}, s32[64,8]{0,1:T(8,128)}, u32[]{:S(2)}) copy-start(s32[64,8]{0,1:T(8,128)} %param.27) | copy-start | bytes 6148
  218.5 65.6 %copy-start.1 = (bf16[64,2048]{1,0:T(8,128)(2,1)S(1)}, bf16[64,2048]{1,0:T(8,128)(2,1)}, u32[]{:S(2)}) copy-start(bf16[64,2048]{1,0:T(8,128)(2,1)} %param.15) | copy-start | bytes 786436
  218.5 67.5 %copy-start.6 = (f32[2048]{0:T(1024)S(1)}, f32[2048]{0:T(1024)}, u32[]{:S(2)}) copy-start(f32[2048]{0:T(1024)} %param.17) | copy-start | bytes 24580
  285.3 0.7 copy-start.2
  287.1 14.8 %all-to-all-start.1 = ((bf16[16,4,2048]{2,1,0:T(4,128)(2,1)}), bf16[16,4,2048]{2,1,0:T(4,128)(2,1)S(1)}, u32[]{:S(2)}, u32[]{:S(2)}) async-start(bf16[16,4,2048]{2,1,0:T(4,128)(2,1)} %reshape.270), calls=%async_computation.2 | async-start | bytes 524288 | tf_op jit(solution)/shard_map/all_to_all | solution.py:180
  308.1 12.3 %all-to-all-start.2 = ((bf16[16,4,2048]{2,1,0:T(4,128)(2,1)}), bf16[16,4,2048]{2,1,0:T(4,128)(2,1)}, u32[]{:S(2)}, u32[]{:S(2)}) async-start(bf16[16,4,2048]{2,1,0:T(4,128)(2,1)} %reshape.272), calls=%async_computation.3 | async-start | bytes 524288 | tf_op jit(solution)/shard_map/all_to_all | solution.py:191
Sparse Core Ops, SparseCore 0:
  10.6 84.6 all-gather.5
  97.7 40.6 all-gather.3
  141.4 72.4 all-gather.7
  218.6 65.4 reduce-scatter.1
